TPU v7x, 32 devices: a whole 2x2x4 slice. The times are simulated.
32 devices in a mesh: seq: 8 (over y, x, core), seg: 4 (over z).
Axes of the slice: x: 2, y: 2, z: 4, core: 2. Of those that a mesh axis runs over, the one named last changes fastest.
Arguments:
- query_rows: bfloat16 [4, 2048, 4, 128], P('seg', 'seq'), may hold values from -6 to 6
- key_rows: bfloat16 [4, 2048, 2, 4, 128], P('seg', 'seq'), may hold values from -6 to 6
- value_rows: bfloat16 [4, 2048, 2, 4, 128], P('seg', 'seq'), may hold values from -6 to 6
- out_gain: float32 [4, 128], replicated, may hold values from 0.5 to 1.5
- initial_state: float32 [4, 128, 128], replicated, may hold values from -24 to 24
Outputs:
- normed_out: bfloat16 [4, 2048, 4, 128], P('seg', 'seq')
All inputs are finite; a program needn't handle non-finite values.
Results may differ from a plain program's by a relative error of at most 0.004.
Values sent between devices are 32-bit elements; how exact they have to be, the bound alone decides.
A program may use at most 128 MiB of HBM per device.

v0:
```python
import jax
import jax.numpy as jnp
from jax import lax
from jax.sharding import PartitionSpec as P

DK = 128
DV = 128
HEADS = 4
REFL = 2
GROUP = 128
highest = lax.Precision.HIGHEST


def carried_in(part, axis, combine, identity):
    place = lax.axis_index(axis)
    gathered = lax.all_gather(part, axis)
    state = jnp.zeros_like(part) + jnp.asarray(identity, part.dtype)

    def one(step, state):
        return combine(state, lax.dynamic_index_in_dim(gathered, step, 0, False))

    return lax.fori_loop(0, place, one, state)


def unit_keys(raw):
    raw = raw.astype(jnp.float32)
    return raw * lax.rsqrt(jnp.sum(raw * raw, axis=-1, keepdims=True) + 1e-06)


def solve_single(matrix, target):
    return jax.scipy.linalg.solve_triangular(matrix, target, lower=True, unit_diagonal=True)


def block_factors(query, keyed, valued):
    steps = keyed.shape[-2]
    tokens = query.shape[-2]
    key_gram = jnp.einsum("...id,...jd->...ij", keyed, keyed, precision=highest)
    lower_unit = jnp.eye(steps, dtype=jnp.float32) + jnp.tril(2.0 * key_gram, -1)
    target = jnp.concatenate([2.0 * keyed, 2.0 * valued], axis=-1)
    flat_lower = lower_unit.reshape(-1, steps, steps)
    flat_target = target.reshape(-1, steps, target.shape[-1])
    solved = jax.vmap(solve_single)(flat_lower, flat_target).reshape(target.shape)
    weights = solved[..., : keyed.shape[-1]]
    updates = solved[..., keyed.shape[-1] :]
    visible = jnp.arange(steps)[None, :] <= REFL * jnp.arange(tokens)[:, None] + (REFL - 1)
    scores = jnp.where(
        visible, jnp.einsum("...td,...ld->...tl", query, keyed, precision=highest), 0.0
    )
    return (weights, updates, scores)


def compose(first_pair, second_pair):
    second_trans = second_pair[..., :DK]
    moved = jnp.einsum("...de,...ef->...df", second_trans, first_pair, precision=highest)
    added = jnp.concatenate([jnp.zeros_like(second_trans), second_pair[..., DK:]], axis=-1)
    return moved + added


def identity_pair():
    eye_part = jnp.broadcast_to(jnp.eye(DK, dtype=jnp.float32), (HEADS, DK, DK))
    return jnp.concatenate([eye_part, jnp.zeros((HEADS, DK, DV), jnp.float32)], axis=-1)


def apply_pair(pair, state):
    return jnp.einsum("hde,hef->hdf", pair[..., :DK], state, precision=highest) + pair[..., DK:]


def ordered_prefix(stacked, position):

    def ordered_accumulate(carry, piece):
        return (compose(carry, piece), carry)

    closing, before_all = lax.scan(ordered_accumulate, identity_pair(), stacked)
    return (lax.dynamic_index_in_dim(before_all, position, 0, keepdims=False), closing)


def per_device(query_rows, key_rows, value_rows, out_gain, initial_state):
    tokens = query_rows.shape[1]
    nblock = tokens // GROUP
    query = (
        query_rows[0].astype(jnp.float32).reshape(nblock, GROUP, HEADS, DK).transpose(0, 2, 1, 3)
    )
    keyed = unit_keys(key_rows[0]).reshape(nblock, GROUP * REFL, HEADS, DK).transpose(0, 2, 1, 3)
    valued = (
        value_rows[0]
        .astype(jnp.float32)
        .reshape(nblock, GROUP * REFL, HEADS, DV)
        .transpose(0, 2, 1, 3)
    )
    weights, updates, scores = block_factors(query, keyed, valued)
    trans_block = jnp.eye(DK, dtype=jnp.float32) - jnp.einsum(
        "chld,chle->chde", keyed, weights, precision=highest
    )
    state_block = jnp.einsum("chld,chle->chde", keyed, updates, precision=highest)
    block_pairs = jnp.concatenate([trans_block, state_block], axis=-1)
    project = query - jnp.einsum("chtl,chld->chtd", scores, weights, precision=highest)
    local_read = jnp.einsum("chtl,chle->chte", scores, updates, precision=highest)

    def body_accumulate(carry, piece):
        return (compose(carry, piece), carry)

    own_pair, before = lax.scan(body_accumulate, identity_pair(), block_pairs)
    reach = jnp.einsum("chtd,chde->chte", project, before[..., :DK], precision=highest)
    base_read = (
        jnp.einsum("chtd,chde->chte", project, before[..., DK:], precision=highest) + local_read
    )
    stacked = lax.all_gather(own_pair[None], "seq", axis=0, tiled=True)
    seq_before, seg_total = ordered_prefix(stacked, lax.axis_index("seq"))
    seg_before = carried_in(seg_total, "seg", compose, identity_pair())
    entry_state = apply_pair(seg_before, initial_state)
    incoming = apply_pair(seq_before, entry_state)
    reads = jnp.einsum("chtd,hde->chte", reach, incoming, precision=highest) + base_read
    reads = reads.transpose(0, 2, 1, 3).reshape(1, tokens, HEADS, DV)
    scale = lax.rsqrt(jnp.mean(reads * reads, axis=-1, keepdims=True) + 1e-06)
    return (reads * scale * out_gain).astype(jnp.bfloat16)


def solution(mesh):
    return jax.shard_map(
        per_device,
        mesh=mesh,
        in_specs=(
            P("seg", "seq", None, None),
            P("seg", "seq", None, None, None),
            P("seg", "seq", None, None, None),
            P(),
            P(),
        ),
        out_specs=P("seg", "seq", None, None),
        check_vma=False,
    )
```

profile of v0, /device:TPU:25, one launch (start us, length us, event | category | flops | bytes accessed | tf_op | source)
XLA Modules:
  0.0 318.8 jit_solution(12129353922683288932)
XLA Ops:
  7.4 1.8 multiply_reduce_fusion
  11.0 1.3 bitcast_multiply_fusion
  12.3 2.3 select_add_fusion
  15.0 5.8 %while.38 = (s32[]{:T(128)}, f32[8,256,256]{2,1,0:T(8,128)S(1)}, s32[2,2]{1,0:T(2,128)S(1)}, f32[2,8,128,128]{3,2,0,1:T(8,128)}, s32[]{:T(128)}) while((s32[]{:T(128)}, f32[8,256,256]{2,1,0:T(8,128)S(1)}, s32[2,2]{1,0:T(2,128)S(1)}, f32[2,8,128,128]{3,2,0,1:T(8,128)}, s32[]{:T(128)}) %tuple.63), condition=%wide.while_cond, body=%wide.while_body.sunk | while | flops 2 | bytes 1049709 | solution.py:31
  15.7 2.2 bitcast_dynamic-update-slice_fusion.8
  18.5 2.2 bitcast_dynamic-update-slice_fusion.8
  20.8 158.6 %custom-call.4 = f32[8,2,128,128]{2,3,1,0:T(8,128)} custom-call(f32[8,2,128,128]{3,2,1,0:T(8,128)} %bitcast.120), custom_call_target="InvertDiagBlocksLowerTriangular" | custom-call | tf_op jit(solution)/shard_map/vmap(jit(_solve_triangular))/triangular_solve | solution.py:31
  179.4 1.8 pad_maximum_fusion
  181.3 1.1 fusion.8
  183.4 1.1 fusion.22
  184.7 2.2 convolution_subtract_fusion.2
  186.9 2.2 fusion.13
  191.0 9.2 %while.35 = (s32[]{:T(128)}, f32[4,128,256]{2,1,0:T(8,128)}, f32[2,4,128,256]{3,2,1,0:T(8,128)}, f32[2,4,128,256]{2,3,1,0:T(8,128)}, s32[]{:T(128)}) while((s32[]{:T(128)}, f32[4,128,256]{2,1,0:T(8,128)}, f32[2,4,128,256]{3,2,1,0:T(8,128)}, f32[2,4,128,256]{2,3,1,0:T(8,128)}, s32[]{:T(128)}) %tuple.66), condition=%wide.region_2.3_spmd, body=%wide.region_1.2_spmd.sunk | while | flops 201457664 | bytes 6291533 | solution.py:102
  194.2 1.4 convolution_add_fusion.9
  198.8 1.4 convolution_add_fusion.9
  200.3 38.0 %all-gather.5.cloned.1.call-done = f32[32,128,256]{2,1,0:T(8,128)} async-done(((f32[4,128,256]{2,1,0:T(8,128)}), f32[32,128,256]{2,1,0:T(8,128)}) %all-gather.5.cloned.1.call-update) | async-done | bytes 4194320 | tf_op jit(solution)/shard_map/all_gather | solution.py:107
  238.4 21.0 %while.36 = (s32[]{:T(128)}, f32[4,128,256]{2,1,0:T(8,128)S(1)}, f32[8,4,128,256]{3,2,1,0:T(8,128)}, f32[8,4,128,256]{3,2,1,0:T(8,128)}, s32[]{:T(128)}) while((s32[]{:T(128)}, f32[4,128,256]{2,1,0:T(8,128)S(1)}, f32[8,4,128,256]{3,2,1,0:T(8,128)}, f32[8,4,128,256]{3,2,1,0:T(8,128)}, s32[]{:T(128)}) %tuple.80), condition=%wide.region_4.5_spmd, body=%wide.region_3.4_spmd.sunk | while | flops 201457664 | bytes 5242957 | solution.py:73
  238.4 1.1 dynamic-slice_bitcast_fusion.5
  241.0 1.1 dynamic-slice_bitcast_fusion.5
  243.7 1.1 dynamic-slice_bitcast_fusion.5
  246.3 1.1 dynamic-slice_bitcast_fusion.5
  248.9 1.1 dynamic-slice_bitcast_fusion.5
  251.5 1.1 dynamic-slice_bitcast_fusion.5
  261.8 2.8 convolution_subtract_fusion.1
  265.9 1.9 fusion.5
  267.8 1.1 dynamic-slice_bitcast_fusion.2
  268.9 34.9 %all-gather.7.cloned.1.call-done = f32[16,128,256]{2,1,0:T(8,128)} async-done(((f32[4,128,256]{2,1,0:T(8,128)}), f32[16,128,256]{2,1,0:T(8,128)}) %all-gather.7.cloned.1.call-update) | async-done | bytes 2097168 | tf_op jit(solution)/shard_map/all_gather | solution.py:16
  303.8 5.3 %while.37 = (s32[]{:T(128)}, f32[4,128,256]{2,1,0:T(8,128)S(1)}, s32[]{:T(128)}, f32[4,4,128,256]{3,2,1,0:T(8,128)}, s32[]{:T(128)}, /*index=5*/s32[]{:T(128)}, s32[]{:T(128)}) while((s32[]{:T(128)}, f32[4,128,256]{2,1,0:T(8,128)S(1)}, s32[]{:T(128)}, f32[4,4,128,256]{3,2,1,0:T(8,128)}, s32[]{:T(128)}, /*index=5*/s32[]{:T(128)}, ...), condition=%wide.region_6.7_spmd, body=%wide.region_5.6_spmd.sunk | while | flops 201457664 | bytes 4194427 | solution.py:22
  303.8 1.1 dynamic-slice_bitcast_fusion.6
  305.6 1.1 dynamic-slice_bitcast_fusion.6
  307.4 1.1 dynamic-slice_bitcast_fusion.6
  310.8 1.1 fusion.26
  (116 shorter events, 35.2 us)
Async XLA Ops:
  6.5 302.6 %copy-start = (f32[4,128,128]{2,1,0:T(8,128)S(1)}, f32[4,128,128]{2,1,0:T(8,128)}, u32[]{:S(2)}) copy-start(f32[4,128,128]{2,1,0:T(8,128)} %param.15) | copy-start | bytes 786436
  6.5 3.1 copy-start.4
  6.5 3.2 copy-start.9
  6.5 231.8 %all-gather.5.cloned.1.call-start = ((), (), s32[]{:S(2)}) async-start(), calls=%async_computation | async-start | bytes 4718592 | tf_op jit(solution)/shard_map/all_gather | solution.py:107
  12.3 2.3 copy-start.7
  179.4 1.9 copy-start.6
  184.7 4.4 %copy-start.2 = (f32[8,256,256]{2,1,0:T(8,128)}, f32[8,256,256]{2,1,0:T(8,128)S(1)}, u32[]{:S(2)}) copy-start(f32[8,256,256]{2,1,0:T(8,128)S(1)} %pad_maximum_fusion.1) | copy-start | bytes 6291460
  200.2 103.6 %all-gather.7.cloned.1.call-start = ((), (), s32[]{:S(2)}) async-start(), calls=%async_computation.1 | async-start | bytes 2621440 | tf_op jit(solution)/shard_map/all_gather | solution.py:16
  238.4 21.9 %copy-start.8 = (bf16[1,256,4,128]{3,2,1,0:T(4,128)(2,1)S(1)}, bf16[1,256,4,128]{3,2,1,0:T(4,128)(2,1)}, u32[]{:S(2)}) copy-start(bf16[1,256,4,128]{3,2,1,0:T(4,128)(2,1)} %param.11) | copy-start | bytes 786436
  259.3 0.8 copy-start.1
  260.2 1.6 copy-start.3
  260.2 4.3 %copy-start.5 = (f32[2,4,128,256]{3,2,1,0:T(8,128)S(1)}, f32[2,4,128,256]{3,2,1,0:T(8,128)}, u32[]{:S(2)}) copy-start(f32[2,4,128,256]{3,2,1,0:T(8,128)} %get-tuple-element.78) | copy-start | bytes 3145732
  309.1 1.7 copy-start.10
Sparse Core Ops, SparseCore 0:
  200.4 37.9 all-gather.4
  260.3 43.4 all-gather.6
where the time goes:
time: 320 us; the launch traced here: 319 us
  other arithmetic  168 us (52%)
  waiting for transfers between devices  73 us (23%)
  local copies, waits for them, and re-layouts  36.5 us (11%)
  matrix products  27.3 us (9%)
  between operations  13.8 us (4%)
    another operation x7, other arithmetic, solve_single(): jax.scipy.linalg.solve_triangular(matrix, target, lower=True, unit_diagon...  160 us
    all_gather x1, waiting for transfers between devices, per_device(): stacked = lax.all_gather(own_pair[None], 'seq', axis=0, tiled=True)  38 us
    all_gather x1, waiting for transfers between devices, carried_in(): gathered = lax.all_gather(part, axis)  34.9 us
    dot_general x13, matrix products, compose(): jnp.einsum('...de,...ef->...df', second_trans, first_pair, precision=high...  9.21 us
    squeeze x8, local copies, waits for them, and re-layouts, ordered_prefix(): closing, before_all = lax.scan(ordered_accumulate, identity_pair(), stacked)  8.7 us
    dynamic_update_slice x8, local copies, waits for them, and re-layouts, ordered_prefix(): closing, before_all = lax.scan(ordered_accumulate, identity_pair(), stacked)  6.85 us
  transfers between devices with their start and end apart: 2, of which 2 were waited for; matrix products, arithmetic and copies ran while one was open for 2% of the time, Pallas kernels for 0%

commit v1 on v0

--- a/solution.py
+++ b/solution.py
@@ -104,7 +104,12 @@
     base_read = (
         jnp.einsum("chtd,chde->chte", project, before[..., DK:], precision=highest) + local_read
     )
-    stacked = lax.all_gather(own_pair[None], "seq", axis=0, tiled=True)
+    ring = [own_pair[None]]
+    for hop in range(7):
+        ring.append(lax.ppermute(ring[-1], "seq", [(dev, (dev + 1) % 8) for dev in range(8)]))
+    stacked = jnp.roll(
+        jnp.concatenate(ring[::-1], axis=0), (lax.axis_index("seq") + 1) * ring[0].shape[0], axis=0
+    )
     seq_before, seg_total = ordered_prefix(stacked, lax.axis_index("seq"))
     seg_before = carried_in(seg_total, "seg", compose, identity_pair())
     entry_state = apply_pair(seg_before, initial_state)

time: 320 us -> 361 us (1.13)
  starting transfers between devices: 0.04 us -> 16.8 us
  waiting for transfers between devices: 73 us -> 84 us
  local copies, waits for them, and re-layouts: 36.5 us -> 46.2 us
    ppermute x0 -> x7, waiting for transfers between devices: none -> 43.2 us  [per_device(): lax.ppermute(ring[-1], 'seq', [(dev, (dev + 1) % 8) for dev in range(8)])]
    all_gather x1 -> x0, waiting for transfers between devices: 38 us -> none  [per_device(): stacked = lax.all_gather(own_pair[None], 'seq', axis=0, tiled=True)]
    ppermute x0 -> x7, starting transfers between devices: none -> 16.8 us  [per_device(): lax.ppermute(ring[-1], 'seq', [(dev, (dev + 1) % 8) for dev in range(8)])]
    unnamed x24 -> x50, local copies, waits for them, and re-layouts: 2.51 us -> 10.2 us
    all_gather x1, waiting for transfers between devices: 34.9 us -> 40.8 us  [carried_in(): gathered = lax.all_gather(part, axis)]
  transfers between devices with their start and end apart: 2 -> 8, of which waited for: 2 -> 8; matrix products, arithmetic and copies ran while one was open for 2% -> 3% of each run, Pallas kernels for 0% -> 0%
where the time goes in v1:
time: 361 us; the launch traced here: 360 us
  other arithmetic  169 us (47%)
  waiting for transfers between devices  84 us (23%)
  local copies, waits for them, and re-layouts  46.2 us (13%)
  matrix products  29.3 us (8%)
  starting transfers between devices  16.8 us (5%)
  between operations  13.9 us (4%)
    another operation x7, other arithmetic, solve_single(): jax.scipy.linalg.solve_triangular(matrix, target, lower=True, unit_diagon...  161 us
    ppermute x7, waiting for transfers between devices, per_device(): lax.ppermute(ring[-1], 'seq', [(dev, (dev + 1) % 8) for dev in range(8)])  43.2 us
    all_gather x1, waiting for transfers between devices, carried_in(): gathered = lax.all_gather(part, axis)  40.8 us
    ppermute x7, starting transfers between devices, per_device(): lax.ppermute(ring[-1], 'seq', [(dev, (dev + 1) % 8) for dev in range(8)])  16.8 us
    unnamed x50, local copies, waits for them, and re-layouts  10.2 us
    squeeze x8, local copies, waits for them, and re-layouts, ordered_prefix(): closing, before_all = lax.scan(ordered_accumulate, identity_pair(), stacked)  8.68 us
    another operation x6, local copies, waits for them, and re-layouts  8.21 us
    dot_general x13, matrix products, compose(): jnp.einsum('...de,...ef->...df', second_trans, first_pair, precision=high...  7.63 us
  transfers between devices with their start and end apart: 8, of which 8 were waited for; matrix products, arithmetic and copies ran while one was open for 3% of the time, Pallas kernels for 0%

profile of v1, /device:TPU:25, one launch (start us, length us, event | category | flops | bytes accessed | tf_op | source)
XLA Modules:
  0.0 359.7 jit_solution(6387729786878931860)
XLA Ops:
  6.6 1.8 multiply_reduce_fusion
  11.3 2.3 select_add_fusion
  15.2 8.2 %while.38 = (s32[]{:T(128)}, f32[8,256,256]{2,1,0:T(8,128)}, s32[2,2]{1,0:T(2,128)S(1)}, f32[2,8,128,128]{3,2,0,1:T(8,128)}, s32[]{:T(128)}) while((s32[]{:T(128)}, f32[8,256,256]{2,1,0:T(8,128)}, s32[2,2]{1,0:T(2,128)S(1)}, f32[2,8,128,128]{3,2,0,1:T(8,128)}, s32[]{:T(128)}) %tuple.63), condition=%wide.while_cond, body=%wide.while_body.sunk | while | flops 2 | bytes 1050209 | solution.py:31
  15.8 3.6 %bitcast_dynamic-update-slice_fusion.8 = f32[2,8,128,128]{3,2,0,1:T(8,128)} fusion(f32[2,8,128,128]{3,2,0,1:T(8,128)} %get-tuple-element.250, s32[]{:T(128)} %get-tuple-element.247, f32[8,256,256]{2,1,0:T(8,128)} %get-tuple-element.253, s32[]{:T(128)} %bitcast.102, s32[]{:T(128)} %bitcast.103), kind=kLoop, calls=%fused_computation.11.clone.1 | loop fusion | bytes 1050112 | tf_op jit(solution)/shard_map/vmap(jit(_solve_triangular))/triangular_solve
  20.0 3.4 bitcast_dynamic-update-slice_fusion.8
  23.4 158.6 %custom-call.4 = f32[8,2,128,128]{2,3,1,0:T(8,128)} custom-call(f32[8,2,128,128]{3,2,1,0:T(8,128)} %bitcast.122), custom_call_target="InvertDiagBlocksLowerTriangular" | custom-call | tf_op jit(solution)/shard_map/vmap(jit(_solve_triangular))/triangular_solve | solution.py:31
  184.9 2.1 convolution_subtract_fusion
  188.4 2.2 fusion.13
  190.6 2.2 convolution_subtract_fusion.2
  194.2 5.6 %while.35 = (s32[]{:T(128)}, f32[4,128,256]{2,1,0:T(8,128)S(1)}, f32[2,4,128,256]{3,2,1,0:T(8,128)}, f32[2,4,128,256]{2,3,1,0:T(8,128)}, s32[]{:T(128)}) while((s32[]{:T(128)}, f32[4,128,256]{2,1,0:T(8,128)S(1)}, f32[2,4,128,256]{3,2,1,0:T(8,128)}, f32[2,4,128,256]{2,3,1,0:T(8,128)}, s32[]{:T(128)}) %tuple.66), condition=%wide.region_2.3_spmd, body=%wide.region_1.2_spmd.sunk | while | flops 201457664 | bytes 6292033 | solution.py:102
  199.8 1.8 collective-permute-start
  201.6 6.1 %collective-permute-done = f32[1,4,128,256]{3,2,1,0:T(8,128)S(1)} collective-permute-done((f32[1,4,128,256]{3,2,1,0:T(8,128)S(1)}, f32[1,4,128,256]{3,2,1,0:T(8,128)S(1)}, u32[]{:S(2)}, u32[]{:S(2)}) %collective-permute-start) | collective-permute-done | bytes 524320 | tf_op jit(solution)/shard_map/ppermute | solution.py:109
  207.7 2.5 collective-permute-start.1
  210.2 6.1 %collective-permute-done.1 = f32[1,4,128,256]{3,2,1,0:T(8,128)S(1)} collective-permute-done((f32[1,4,128,256]{3,2,1,0:T(8,128)S(1)}, f32[1,4,128,256]{3,2,1,0:T(8,128)S(1)}, u32[]{:S(2)}, u32[]{:S(2)}) %collective-permute-start.1) | collective-permute-done | bytes 524320 | tf_op jit(solution)/shard_map/ppermute | solution.py:109
  216.4 2.5 collective-permute-start.2
  218.8 6.1 %collective-permute-done.2 = f32[1,4,128,256]{3,2,1,0:T(8,128)S(1)} collective-permute-done((f32[1,4,128,256]{3,2,1,0:T(8,128)S(1)}, f32[1,4,128,256]{3,2,1,0:T(8,128)S(1)}, u32[]{:S(2)}, u32[]{:S(2)}) %collective-permute-start.2) | collective-permute-done | bytes 524320 | tf_op jit(solution)/shard_map/ppermute | solution.py:109
  225.8 2.5 collective-permute-start.3
  228.2 6.1 %collective-permute-done.3 = f32[1,4,128,256]{3,2,1,0:T(8,128)S(1)} collective-permute-done((f32[1,4,128,256]{3,2,1,0:T(8,128)S(1)}, f32[1,4,128,256]{3,2,1,0:T(8,128)S(1)}, u32[]{:S(2)}, u32[]{:S(2)}) %collective-permute-start.3) | collective-permute-done | bytes 524320 | tf_op jit(solution)/shard_map/ppermute | solution.py:109
  235.2 2.5 collective-permute-start.4
  237.7 6.1 %collective-permute-done.4 = f32[1,4,128,256]{3,2,1,0:T(8,128)S(1)} collective-permute-done((f32[1,4,128,256]{3,2,1,0:T(8,128)S(1)}, f32[1,4,128,256]{3,2,1,0:T(8,128)S(1)}, u32[]{:S(2)}, u32[]{:S(2)}) %collective-permute-start.4) | collective-permute-done | bytes 524320 | tf_op jit(solution)/shard_map/ppermute | solution.py:109
  244.6 2.5 collective-permute-start.5
  247.1 6.1 %collective-permute-done.5 = f32[1,4,128,256]{3,2,1,0:T(8,128)} collective-permute-done((f32[1,4,128,256]{3,2,1,0:T(8,128)S(1)}, f32[1,4,128,256]{3,2,1,0:T(8,128)}, u32[]{:S(2)}, u32[]{:S(2)}) %collective-permute-start.5) | collective-permute-done | bytes 524320 | tf_op jit(solution)/shard_map/ppermute | solution.py:109
  253.2 2.6 collective-permute-start.6
  255.8 6.4 %collective-permute-done.6 = f32[1,4,128,256]{3,2,1,0:T(8,128)} collective-permute-done((f32[1,4,128,256]{3,2,1,0:T(8,128)}, f32[1,4,128,256]{3,2,1,0:T(8,128)}, u32[]{:S(2)}, u32[]{:S(2)}) %collective-permute-start.6) | collective-permute-done | bytes 524320 | tf_op jit(solution)/shard_map/ppermute | solution.py:109
  269.4 2.3 constant_dynamic-slice_fusion.2
  271.7 21.0 %while.36 = (s32[]{:T(128)}, f32[4,128,256]{2,1,0:T(8,128)S(1)}, f32[8,4,128,256]{3,2,1,0:T(8,128)}, f32[8,4,128,256]{3,2,1,0:T(8,128)}, s32[]{:T(128)}) while((s32[]{:T(128)}, f32[4,128,256]{2,1,0:T(8,128)S(1)}, f32[8,4,128,256]{3,2,1,0:T(8,128)}, f32[8,4,128,256]{3,2,1,0:T(8,128)}, s32[]{:T(128)}) %tuple.78), condition=%wide.region_4.5_spmd, body=%wide.region_3.4_spmd.sunk | while | flops 201457664 | bytes 5243457 | solution.py:73
  294.4 3.1 convolution_subtract_fusion.1
  297.5 1.7 fusion.19
  299.2 1.7 fusion.23
  300.9 1.9 fusion.5
  303.9 40.8 %all-gather.3.cloned.1.call-done = f32[16,128,256]{2,1,0:T(8,128)} async-done(((f32[4,128,256]{2,1,0:T(8,128)}), f32[16,128,256]{2,1,0:T(8,128)}) %all-gather.3.cloned.1.call-update) | async-done | bytes 2097168 | tf_op jit(solution)/shard_map/all_gather | solution.py:16
  344.6 5.3 %while.37 = (s32[]{:T(128)}, f32[4,128,256]{2,1,0:T(8,128)S(1)}, s32[]{:T(128)}, f32[4,4,128,256]{3,2,1,0:T(8,128)}, s32[]{:T(128)}, /*index=5*/s32[]{:T(128)}, s32[]{:T(128)}) while((s32[]{:T(128)}, f32[4,128,256]{2,1,0:T(8,128)S(1)}, s32[]{:T(128)}, f32[4,4,128,256]{3,2,1,0:T(8,128)}, s32[]{:T(128)}, /*index=5*/s32[]{:T(128)}, ...), condition=%wide.region_6.7_spmd, body=%wide.region_5.6_spmd.sunk | while | flops 201457664 | bytes 4194419 | solution.py:22
  (155 shorter events, 57.5 us)
Async XLA Ops:
  6.5 343.4 %copy-start = (f32[4,128,128]{2,1,0:T(8,128)S(1)}, f32[4,128,128]{2,1,0:T(8,128)}, u32[]{:S(2)}) copy-start(f32[4,128,128]{2,1,0:T(8,128)} %param.15) | copy-start | bytes 786436
  6.5 338.1 %all-gather.3.cloned.1.call-start = ((), (), s32[]{:S(2)}) async-start(), calls=%async_computation | async-start | bytes 2621440 | tf_op jit(solution)/shard_map/all_gather | solution.py:16
  13.6 168.5 %copy-start.15 = (bf16[1,256,2,4,128]{4,3,2,1,0:T(4,128)(2,1)S(1)}, bf16[1,256,2,4,128]{4,3,2,1,0:T(4,128)(2,1)}, u32[]{:S(2)}) copy-start(bf16[1,256,2,4,128]{4,3,2,1,0:T(4,128)(2,1)} %param.13) | copy-start | bytes 1572868
  182.1 1.8 copy-start.13
  188.4 2.2 copy-start.5
  193.0 62.8 %copy-start.1 = (f32[4,128,256]{2,1,0:T(8,128)}, f32[4,128,256]{2,1,0:T(8,128)S(1)}, u32[]{:S(2)}) copy-start(f32[4,128,256]{2,1,0:T(8,128)S(1)} %concatenate.29) | copy-start | bytes 1572868
  199.8 7.9 %collective-permute-start = (f32[1,4,128,256]{3,2,1,0:T(8,128)S(1)}, f32[1,4,128,256]{3,2,1,0:T(8,128)S(1)}, u32[]{:S(2)}, u32[]{:S(2)}) collective-permute-start(f32[1,4,128,256]{3,2,1,0:T(8,128)S(1)} %bitcast.106), channel_id=1, source_target_pairs={{0,4},{4,8},{8,12},{12,16},{16,20},{20,24},{24,28},{28,0},{1,5},{5... | collective-permute-start | bytes 1572872 | tf_op jit(solution)/shard_map/ppermute | solution.py:109
  207.7 8.6 %collective-permute-start.1 = (f32[1,4,128,256]{3,2,1,0:T(8,128)S(1)}, f32[1,4,128,256]{3,2,1,0:T(8,128)S(1)}, u32[]{:S(2)}, u32[]{:S(2)}) collective-permute-start(f32[1,4,128,256]{3,2,1,0:T(8,128)S(1)} %collective-permute-done), channel_id=1, source_target_pairs={{0,4},{4,8},{8,12},{12,16},{16,20},{20,24},{24,28},{28,0},{1,5},{5... | collective-permute-start | bytes 1572872 | tf_op jit(solution)/shard_map/ppermute | solution.py:109
  216.4 8.6 %collective-permute-start.2 = (f32[1,4,128,256]{3,2,1,0:T(8,128)S(1)}, f32[1,4,128,256]{3,2,1,0:T(8,128)S(1)}, u32[]{:S(2)}, u32[]{:S(2)}) collective-permute-start(f32[1,4,128,256]{3,2,1,0:T(8,128)S(1)} %collective-permute-done.1), channel_id=1, source_target_pairs={{0,4},{4,8},{8,12},{12,16},{16,20},{20,24},{24,28},{28,0},{1,5},{5... | collective-permute-start | bytes 1572872 | tf_op jit(solution)/shard_map/ppermute | solution.py:109
  225.0 0.8 copy-start.7
  225.8 8.6 %collective-permute-start.3 = (f32[1,4,128,256]{3,2,1,0:T(8,128)S(1)}, f32[1,4,128,256]{3,2,1,0:T(8,128)S(1)}, u32[]{:S(2)}, u32[]{:S(2)}) collective-permute-start(f32[1,4,128,256]{3,2,1,0:T(8,128)S(1)} %collective-permute-done.2), channel_id=1, source_target_pairs={{0,4},{4,8},{8,12},{12,16},{16,20},{20,24},{24,28},{28,0},{1,5},{5... | collective-permute-start | bytes 1572872 | tf_op jit(solution)/shard_map/ppermute | solution.py:109
  234.4 0.8 copy-start.9
  235.2 8.6 %collective-permute-start.4 = (f32[1,4,128,256]{3,2,1,0:T(8,128)S(1)}, f32[1,4,128,256]{3,2,1,0:T(8,128)S(1)}, u32[]{:S(2)}, u32[]{:S(2)}) collective-permute-start(f32[1,4,128,256]{3,2,1,0:T(8,128)S(1)} %collective-permute-done.3), channel_id=1, source_target_pairs={{0,4},{4,8},{8,12},{12,16},{16,20},{20,24},{24,28},{28,0},{1,5},{5... | collective-permute-start | bytes 1572872 | tf_op jit(solution)/shard_map/ppermute | solution.py:109
  243.8 0.8 copy-start.11
  244.6 8.6 %collective-permute-start.5 = (f32[1,4,128,256]{3,2,1,0:T(8,128)S(1)}, f32[1,4,128,256]{3,2,1,0:T(8,128)}, u32[]{:S(2)}, u32[]{:S(2)}) collective-permute-start(f32[1,4,128,256]{3,2,1,0:T(8,128)S(1)} %collective-permute-done.4), channel_id=1, source_target_pairs={{0,4},{4,8},{8,12},{12,16},{16,20},{20,24},{24,28},{28,0},{1,5},{5... | collective-permute-start | bytes 1572872 | tf_op jit(solution)/shard_map/ppermute | solution.py:109
  253.2 9.0 %collective-permute-start.6 = (f32[1,4,128,256]{3,2,1,0:T(8,128)}, f32[1,4,128,256]{3,2,1,0:T(8,128)}, u32[]{:S(2)}, u32[]{:S(2)}) collective-permute-start(f32[1,4,128,256]{3,2,1,0:T(8,128)} %collective-permute-done.5), channel_id=1, source_target_pairs={{0,4},{4,8},{8,12},{12,16},{16,20},{20,24},{24,28},{28,0},{1,5},{5... | collective-permute-start | bytes 1572872 | tf_op jit(solution)/shard_map/ppermute | solution.py:109
  255.8 10.9 %copy-start.8 = (f32[1,4,128,256]{3,2,1,0:T(8,128)S(1)}, f32[1,4,128,256]{3,2,1,0:T(8,128)}, u32[]{:S(2)}) copy-start(f32[1,4,128,256]{3,2,1,0:T(8,128)} %copy-done.7) | copy-start | bytes 1572868
  264.4 4.7 %copy-start.12 = (f32[1,4,128,256]{3,2,1,0:T(8,128)S(1)}, f32[1,4,128,256]{3,2,1,0:T(8,128)}, u32[]{:S(2)}) copy-start(f32[1,4,128,256]{3,2,1,0:T(8,128)} %copy-done.11) | copy-start | bytes 1572868
  265.5 3.6 copy-start.10
  269.3 2.3 copy-start.4
  271.7 21.9 %copy-start.14 = (bf16[1,256,4,128]{3,2,1,0:T(4,128)(2,1)S(1)}, bf16[1,256,4,128]{3,2,1,0:T(4,128)(2,1)}, u32[]{:S(2)}) copy-start(bf16[1,256,4,128]{3,2,1,0:T(4,128)(2,1)} %param.11) | copy-start | bytes 786436
  292.7 0.8 copy-start.3
  293.6 7.3 %copy-start.6 = (f32[8,256,256]{2,1,0:T(8,128)S(1)}, f32[8,256,256]{2,1,0:T(8,128)}, u32[]{:S(2)}) copy-start(f32[8,256,256]{2,1,0:T(8,128)} %copy-done.5) | copy-start | bytes 6291460
  297.5 47.2 %copy-start.2 = (f32[4,128,256]{2,1,0:T(8,128)S(1)}, f32[4,128,256]{2,1,0:T(8,128)}, u32[]{:S(2)}) copy-start(f32[4,128,256]{2,1,0:T(8,128)} %copy-done.1) | copy-start | bytes 1572868
  344.6 7.1 %copy-start.16 = (f32[4,128]{1,0:T(4,128)S(1)}, f32[4,128]{1,0:T(4,128)}, u32[]{:S(2)}) copy-start(f32[4,128]{1,0:T(4,128)} %param.14) | copy-start | bytes 6148
Sparse Core Ops, SparseCore 0:
  293.7 50.9 all-gather.2
